TPU v7x, 32 devices: a whole 2x2x4 slice. The times are simulated.
32 devices in a mesh: rep: 4 (over y, x), fsdp: 4 (over z), ctx: 2 (over core).
Axes of the slice: x: 2, y: 2, z: 4, core: 2. Of those that a mesh axis runs over, the one named last changes fastest.
Arguments:
- inputs: bfloat16 [2, 16, 1024, 768], P(None, ('rep', 'fsdp'), 'ctx'), may hold values from -6 to 6
- weight_qkv: bfloat16 [768, 2304], P('fsdp'), may hold values from -0.21875 to 0.21875
- bias_query: bfloat16 [768], P('fsdp'), may hold values from -3 to 3
- bias_value: bfloat16 [768], P('fsdp'), may hold values from -3 to 3
- weight_mix: bfloat16 [768, 768], P('fsdp'), may hold values from -1.75 to 1.75
- bias_mix: bfloat16 [768], P('fsdp'), may hold values from -2 to 2
- gain_attn: bfloat16 [768], P('fsdp'), may hold values from 0.099609375 to 1.8984375
- shift_attn: bfloat16 [768], P('fsdp'), may hold values from -2 to 2
- gain_mlp: bfloat16 [768], P('fsdp'), may hold values from 0.099609375 to 1.8984375
- shift_mlp: bfloat16 [768], P('fsdp'), may hold values from -2 to 2
- weight_up: bfloat16 [768, 3072], P('fsdp'), may hold values from -0.21875 to 0.21875
- bias_up: bfloat16 [3072], P('fsdp'), may hold values from -3 to 3
- weight_down: bfloat16 [3072, 768], P('fsdp'), may hold values from -0.109375 to 0.109375
- bias_down: bfloat16 [768], P('fsdp'), may hold values from -2 to 2
- cotangent: bfloat16 [2, 16, 1024, 768], P(None, ('rep', 'fsdp'), 'ctx'), may hold values from -6 to 6
Outputs:
- outputs: bfloat16 [2, 16, 1024, 768], P(None, ('rep', 'fsdp'), 'ctx')
- grad_inputs: float32 [2, 16, 1024, 768], P(None, ('rep', 'fsdp'), 'ctx')
- weight_qkv_grad: float32 [768, 2304], P('fsdp')
- bias_query_grad: float32 [768], P('fsdp')
- bias_value_grad: float32 [768], P('fsdp')
- weight_mix_grad: float32 [768, 768], P('fsdp')
- bias_mix_grad: float32 [768], P('fsdp')
- gain_attn_grad: float32 [768], P('fsdp')
- shift_attn_grad: float32 [768], P('fsdp')
- gain_mlp_grad: float32 [768], P('fsdp')
- shift_mlp_grad: float32 [768], P('fsdp')
- weight_up_grad: float32 [768, 3072], P('fsdp')
- bias_up_grad: float32 [3072], P('fsdp')
- weight_down_grad: float32 [3072, 768], P('fsdp')
- bias_down_grad: float32 [768], P('fsdp')
All inputs are finite; a program needn't handle non-finite values.
Results may differ from a plain program's by a relative error of at most 0.018.
Values may be sent and summed in bfloat16 or wider, within the bound.
A program may use at most 320 MiB of HBM per device.

v0:
```python
from functools import partial
import jax
import jax.numpy as jnp
from jax import lax
from jax.sharding import PartitionSpec as P

H = 12
EPS = 1e-05


def from_behind(x, axis, by):
    peers = lax.axis_size(axis)
    pairs = [(i, i + by) for i in range(peers) if 0 <= i + by < peers]
    return lax.ppermute(x, axis, pairs)


def for_sending(x):

    def short(part):
        return part.astype(jnp.bfloat16) if part.dtype == jnp.float32 else part

    return jax.tree.map(short, x)


def norm_stats(values):
    center = values - jnp.mean(values, axis=-1, keepdims=True)
    inverse = lax.rsqrt(jnp.mean(center * center, axis=-1, keepdims=True) + EPS)
    return (center * inverse, inverse)


def norm_back(grad_norm, normal, inverse, gain):
    scaled = grad_norm * gain
    return inverse * (
        scaled
        - jnp.mean(scaled, axis=-1, keepdims=True)
        - normal * jnp.mean(scaled * normal, axis=-1, keepdims=True)
    )


def column_sum(values):
    return jnp.sum(values.astype(jnp.float32), axis=(0, 1))


def outer_sum(left, right):
    return jnp.einsum("sri,srj->ij", left, right, preferred_element_type=jnp.float32)


def project(left, weight):
    return jnp.einsum("sri,ij->srj", left, weight, preferred_element_type=jnp.float32)


def project_back(grad_rows, weight):
    return jnp.einsum("srj,ij->sri", grad_rows, weight, preferred_element_type=jnp.float32)


def split_heads(values):
    return values.reshape(values.shape[0], values.shape[1], H, values.shape[2] // H)


def attention_scores(query_heads, key_heads, allowed, factor):
    raw = jnp.einsum("sqhd,skhd->shqk", query_heads, key_heads, preferred_element_type=jnp.float32)
    return jnp.where(allowed, raw * factor, -1e30)


def local(
    inputs,
    weight_qkv,
    bias_query,
    bias_value,
    weight_mix,
    bias_mix,
    gain_attn,
    shift_attn,
    gain_mlp,
    shift_mlp,
    weight_up,
    bias_up,
    weight_down,
    bias_down,
    cotangent,
):
    shards = (
        weight_qkv,
        bias_query,
        bias_value,
        weight_mix,
        bias_mix,
        gain_attn,
        shift_attn,
        gain_mlp,
        shift_mlp,
        weight_up,
        bias_up,
        weight_down,
        bias_down,
    )
    width = weight_qkv.shape[1] // 3
    factor = (width // H) ** (-0.5)
    rows = inputs.shape[2]
    owners = lax.axis_size("fsdp")
    ctx_index = lax.axis_index("ctx")
    query_pos = lax.broadcasted_iota(jnp.int32, (rows, 2 * rows), 0)
    key_pos = lax.broadcasted_iota(jnp.int32, (rows, 2 * rows), 1) - rows
    allowed = (key_pos <= query_pos) & ((key_pos >= 0) | (ctx_index > 0))
    whole_zeros = tuple(
        (jnp.zeros((item.shape[0] * owners,) + item.shape[1:], jnp.float32) for item in shards)
    )
    bf16 = jnp.bfloat16
    f32 = jnp.float32

    def micro(totals, pair):
        tokens_in, grad_in = pair
        full = (
            lax.all_gather(shards[0], "fsdp", axis=0, tiled=True),
            lax.all_gather(shards[1], "fsdp", axis=0, tiled=True),
            lax.all_gather(shards[2], "fsdp", axis=0, tiled=True),
            lax.all_gather(shards[3], "fsdp", axis=0, tiled=True),
            lax.all_gather(shards[4], "fsdp", axis=0, tiled=True),
            lax.all_gather(shards[5], "fsdp", axis=0, tiled=True),
            lax.all_gather(shards[6], "fsdp", axis=0, tiled=True),
            lax.all_gather(shards[7], "fsdp", axis=0, tiled=True),
            lax.all_gather(shards[8], "fsdp", axis=0, tiled=True),
            lax.all_gather(shards[9], "fsdp", axis=0, tiled=True),
            lax.all_gather(shards[10], "fsdp", axis=0, tiled=True),
            lax.all_gather(shards[11], "fsdp", axis=0, tiled=True),
            lax.all_gather(shards[12], "fsdp", axis=0, tiled=True),
        )
        tokens = tokens_in.astype(f32)
        normal_one, inverse_one = norm_stats(tokens)
        first = (normal_one * full[5] + full[6]).astype(bf16)
        joined = project(first, full[0])
        query = (joined[..., :width] + full[1]).astype(bf16)
        key_own = joined[..., width : 2 * width].astype(bf16)
        value_own = (joined[..., 2 * width :] + full[2]).astype(bf16)
        key_prev, value_prev = from_behind((key_own, value_own), "ctx", 1)
        key_heads = split_heads(jnp.concatenate([key_prev, key_own], axis=1))
        value_heads = split_heads(jnp.concatenate([value_prev, value_own], axis=1))
        query_heads = split_heads(query)
        scores = attention_scores(query_heads, key_heads, allowed, factor)
        top = jnp.max(scores, axis=-1, keepdims=True)
        logsum = top + jnp.log(jnp.sum(jnp.exp(scores - top), axis=-1, keepdims=True))
        probs_low = jnp.exp(scores - logsum).astype(bf16)
        mixed = jnp.einsum("shqk,skhd->sqhd", probs_low, value_heads, preferred_element_type=f32)
        mixed = mixed.reshape(tokens.shape).astype(bf16)
        middle = tokens + project(mixed, full[3]) + full[4]
        normal_two, inverse_two = norm_stats(middle)
        second = (normal_two * full[7] + full[8]).astype(bf16)
        before = project(second, full[9]) + full[10]
        active = jax.nn.gelu(before, approximate=True).astype(bf16)
        result = (middle + project(active, full[11]) + full[12]).astype(bf16)
        again = (
            lax.all_gather(shards[0], "fsdp", axis=0, tiled=True),
            lax.all_gather(shards[1], "fsdp", axis=0, tiled=True),
            lax.all_gather(shards[2], "fsdp", axis=0, tiled=True),
            lax.all_gather(shards[3], "fsdp", axis=0, tiled=True),
            lax.all_gather(shards[4], "fsdp", axis=0, tiled=True),
            lax.all_gather(shards[5], "fsdp", axis=0, tiled=True),
            lax.all_gather(shards[6], "fsdp", axis=0, tiled=True),
            lax.all_gather(shards[7], "fsdp", axis=0, tiled=True),
            lax.all_gather(shards[8], "fsdp", axis=0, tiled=True),
            lax.all_gather(shards[9], "fsdp", axis=0, tiled=True),
            lax.all_gather(shards[10], "fsdp", axis=0, tiled=True),
            lax.all_gather(shards[11], "fsdp", axis=0, tiled=True),
            lax.all_gather(shards[12], "fsdp", axis=0, tiled=True),
        )
        grad_out = grad_in.astype(f32)
        d_down = grad_out.astype(bf16)
        g_wdown = outer_sum(active, d_down)
        g_bdown = column_sum(d_down)
        d_active = project_back(d_down, again[11])
        gelu_back = jax.vjp(partial(jax.nn.gelu, approximate=True), before)[1]
        d_before = gelu_back(d_active)[0].astype(bf16)
        g_wup = outer_sum(second, d_before)
        g_bup = column_sum(d_before)
        d_second = project_back(d_before, again[9])
        g_gmlp = jnp.sum(d_second * normal_two, axis=(0, 1))
        g_smlp = jnp.sum(d_second, axis=(0, 1))
        d_middle = grad_out + norm_back(d_second, normal_two, inverse_two, again[7])
        d_branch = d_middle.astype(bf16)
        g_wmix = outer_sum(mixed, d_branch)
        g_bmix = column_sum(d_branch)
        d_mixed = split_heads(project_back(d_branch, again[3]).astype(bf16))
        scores = attention_scores(query_heads, key_heads, allowed, factor)
        probs = jnp.exp(scores - logsum)
        probs_low = probs.astype(bf16)
        d_probs = jnp.einsum("sqhd,skhd->shqk", d_mixed, value_heads, preferred_element_type=f32)
        d_scores = (
            probs * (d_probs - jnp.sum(d_probs * probs, axis=-1, keepdims=True)) * factor
        ).astype(bf16)
        d_query = jnp.einsum("shqk,skhd->sqhd", d_scores, key_heads, preferred_element_type=f32)
        d_query = d_query.reshape(tokens.shape).astype(bf16)
        d_key_all = jnp.einsum("shqk,sqhd->skhd", d_scores, query_heads, preferred_element_type=f32)
        d_value_all = jnp.einsum("shqk,sqhd->skhd", probs_low, d_mixed, preferred_element_type=f32)
        d_key_all = d_key_all.reshape(tokens.shape[0], 2 * rows, width)
        d_value_all = d_value_all.reshape(tokens.shape[0], 2 * rows, width)
        key_back, value_back = (
            from_behind(d_key_all[:, :rows].astype(jnp.bfloat16), "ctx", -1).astype(jnp.float32),
            from_behind(d_value_all[:, :rows].astype(jnp.bfloat16), "ctx", -1).astype(jnp.float32),
        )
        d_key = (d_key_all[:, rows:] + key_back).astype(bf16)
        d_value = (d_value_all[:, rows:] + value_back).astype(bf16)
        d_joined = jnp.concatenate([d_query, d_key, d_value], axis=-1)
        g_wqkv = outer_sum(first, d_joined)
        g_bquery = column_sum(d_query)
        g_bvalue = column_sum(d_value)
        d_first = project_back(d_joined, again[0])
        g_gattn = jnp.sum(d_first * normal_one, axis=(0, 1))
        g_sattn = jnp.sum(d_first, axis=(0, 1))
        d_tokens = d_middle + norm_back(d_first, normal_one, inverse_one, again[5])
        terms = (
            g_wqkv,
            g_bquery,
            g_bvalue,
            g_wmix,
            g_bmix,
            g_gattn,
            g_sattn,
            g_gmlp,
            g_smlp,
            g_wup,
            g_bup,
            g_wdown,
            g_bdown,
        )
        totals = tuple((left + right for left, right in zip(totals, terms)))
        return (totals, (result, d_tokens))

    totals, (results, grad_tokens) = lax.scan(micro, whole_zeros, (inputs, cotangent))
    shares = jax.tree.map(
        lambda part: part.astype(jnp.float32),
        lax.psum_scatter(for_sending(totals), "fsdp", scatter_dimension=0, tiled=True),
    )
    summed = jax.tree.map(
        lambda part: part.astype(jnp.float32), lax.psum(for_sending(shares), ("rep", "ctx"))
    )
    return (results, grad_tokens) + tuple(summed)


def solution(mesh):
    in_specs = (
        P(None, ("rep", "fsdp"), "ctx", None),
        P("fsdp", None),
        P("fsdp"),
        P("fsdp"),
        P("fsdp", None),
        P("fsdp"),
        P("fsdp"),
        P("fsdp"),
        P("fsdp"),
        P("fsdp"),
        P("fsdp", None),
        P("fsdp"),
        P("fsdp", None),
        P("fsdp"),
        P(None, ("rep", "fsdp"), "ctx", None),
    )
    out_specs = (
        P(None, ("rep", "fsdp"), "ctx", None),
        P(None, ("rep", "fsdp"), "ctx", None),
        P("fsdp", None),
        P("fsdp"),
        P("fsdp"),
        P("fsdp", None),
        P("fsdp"),
        P("fsdp"),
        P("fsdp"),
        P("fsdp"),
        P("fsdp"),
        P("fsdp", None),
        P("fsdp"),
        P("fsdp", None),
        P("fsdp"),
    )
    return jax.shard_map(local, mesh=mesh, in_specs=in_specs, out_specs=out_specs, check_vma=False)
```

profile of v0, /device:TPU:0, one launch (start us, length us, event | category | flops | bytes accessed | tf_op | source)
XLA Modules:
  0.0 1352.4 jit_solution(5778753269937234375)
XLA Ops:
  8.2 974.8 %while.41 = (s32[]{:T(128)}, f32[768,2304]{1,0:T(8,128)}, f32[768]{0:T(1024)}, f32[768]{0:T(1024)}, f32[768,768]{1,0:T(8,128)}, /*index=5*/f32[768]{0:T(1024)}, ...) while((s32[]{:T(128)}, f32[768,2304]{1,0:T(8,128)}, ...), condition=%wide.region_21.22_spmd.clone, body=%wide.region_0.21_spmd.clone.sunk | while | flops 26950144000 | bytes 699213696 | solution.py:228
  19.6 21.4 %all-reduce.30 = (bf16[768]{0:T(1024)(128)(2,1)S(1)}, bf16[768]{0:T(1024)(128)(2,1)S(1)}, bf16[768]{0:T(1024)(128)(2,1)S(1)}, bf16[768]{0:T(1024)(128)(2,1)S(1)}...) all-reduce(bf16[768]{0:T(1024)(128)(2,1)S(1)} %dynamic-update-slice, ...), channel_id=1, replica_groups=mesh['rep'=4,'fsdp'=4,'ctx'=2] {'fsdp'}, use_global_device_ids=true, to_apply=%add.1 | all-reduce | flops 6144 | bytes 24576 | tf_op jit(solution)/shard_map/while
  42.7 41.6 %all-gather.11.cloned.1.call-done = bf16[768,2304]{1,0:T(8,128)(2,1)} async-done(((bf16[192,2304]{1,0:T(8,128)(2,1)}), bf16[768,2304]{1,0:T(8,128)(2,1)}) %all-gather.11.cloned.1.call-update) | async-done | bytes 3538960 | tf_op jit(solution)/shard_map/while/body/eval_jaxpr/all_gather | solution.py:114
  84.3 4.2 convolution_bitcast_fusion.2
  88.8 2.7 collective-permute-start
  94.7 13.2 all-gather.3
  116.7 15.2 %fusion.201 = (f32[12,512]{1,0:T(8,128)S(1)}, f32[12,512,1024]{2,1,0:T(8,128)}) fusion(pred[512,1024]{1,0:T(8,128)(4,1)} %fusion.200, bf16[512,12,64]{0,2,1:T(8,128)(2,1)} %bitcast.212, bf16[1024,12,64]{0,2,1:T(8,128)(2,1)} %bitcast.210), kind=kOutput, calls=%fused_computation.8.clone.1 | convolution fusion | flops 824174592 | bytes 28073984 | tf_op jit(solution)/shard_map/while/body/eval_jaxpr/sqhd,skhd->shqk/dot_general | solution.py:61
  131.9 11.8 exponential_reduce_fusion.2
  143.8 12.1 convolution_convert_fusion.4
  155.9 2.7 fusion.202
  158.9 46.3 %all-gather.13.cloned.1.call-done = bf16[768,3072]{1,0:T(8,128)(2,1)} async-done(((bf16[192,3072]{1,0:T(8,128)(2,1)}), bf16[768,3072]{1,0:T(8,128)(2,1)}) %all-gather.13.cloned.1.call-update) | async-done | bytes 4718608 | tf_op jit(solution)/shard_map/while/body/eval_jaxpr/all_gather | solution.py:123
  205.2 7.1 fusion.203
  212.3 82.2 %all-gather.15.cloned.1.call-done = bf16[3072,768]{1,0:T(8,128)(2,1)} async-done(((bf16[768,768]{1,0:T(8,128)(2,1)}), bf16[3072,768]{1,0:T(8,128)(2,1)}) %all-gather.15.cloned.1.call-update) | async-done | bytes 4718608 | tf_op jit(solution)/shard_map/while/body/eval_jaxpr/all_gather | solution.py:163
  294.5 9.3 convert_reduce_fusion.13
  303.8 3.0 multiply_reduce_fusion.9
  309.9 2.3 copy.53
  312.2 13.6 %fusion.204 = f32[12,64,1024]{2,1,0:T(8,128)} fusion(bf16[512,12,64]{0,2,1:T(8,128)(2,1)} %bitcast.208, f32[12,512]{1,0:T(8,128)S(1)} %log_add_fusion.2, f32[12,512,1024]{2,1,0:T(8,128)} %get-tuple-element.914, pred[512,1024]{1,0:T(8,128)(4,1)} %fusion.200), kind=kOutput, calls=%fused_computation.107.clone.1 | convolution fusion | flops 830472192 | bytes 29646848 | tf_op jit(solution)/shard_map/while/body/eval_jaxpr/shqk,sqhd->skhd/dot_general | solution.py:193
  325.8 10.1 fusion.205
  335.9 52.3 %convert_reduce_fusion.16 = (f32[12,64]{1,0:T(8,128)S(1)}, bf16[12,64,512]{2,1,0:T(8,128)(2,1)}) fusion(bf16[1024,12,64]{0,2,1:T(8,128)(2,1)} %bitcast.211, f32[12,512,1024]{2,1,0:T(8,128)} %fusion.205, f32[12,512]{1,0:T(8,128)S(1)} %log_add_fusion.2, f32[12,512,1024]{2,1,0:T(8,128)} %get-tuple-element.914, pred[512,1024]{1,0:T(8,128)(4,1)} %fusion.200), kind=kOutput, calls=%fused_computation.77.clone.1 | convolution fusion | flops 875698432 | bytes 53242880 | tf_op jit(solution)/shard_map/while/body/eval_jaxpr/shqk,skhd->sqhd/dot_general | solution.py:190
  388.2 54.3 %fusion.206 = f32[12,64,1024]{2,1,0:T(8,128)} fusion(bf16[512,12,64]{0,2,1:T(8,128)(2,1)} %bitcast.213, f32[12,512,1024]{2,1,0:T(8,128)} %fusion.205, f32[12,512]{1,0:T(8,128)S(1)} %log_add_fusion.2, f32[12,512,1024]{2,1,0:T(8,128)} %get-tuple-element.914, pred[512,1024]{1,0:T(8,128)(4,1)} %fusion.200), kind=kOutput, calls=%fused_computation.10.clone.1 | convolution fusion | flops 874519552 | bytes 54812672 | tf_op jit(solution)/shard_map/while/body/eval_jaxpr/shqk,sqhd->skhd/dot_general | solution.py:192
  442.5 10.5 select_add_fusion.31
  453.0 2.4 slice.86
  456.7 5.6 select_add_fusion.29
  465.2 9.1 fusion.209
  476.3 2.5 convert_reduce_fusion.15
  479.5 7.3 select_add_fusion.23
  486.8 2.7 fusion.208
  502.7 16.6 %all-reduce.30 = (bf16[768]{0:T(1024)(128)(2,1)S(1)}, bf16[768]{0:T(1024)(128)(2,1)S(1)}, bf16[768]{0:T(1024)(128)(2,1)S(1)}, bf16[768]{0:T(1024)(128)(2,1)S(1)}...) all-reduce(bf16[768]{0:T(1024)(128)(2,1)S(1)} %dynamic-update-slice, ...), channel_id=1, replica_groups=mesh['rep'=4,'fsdp'=4,'ctx'=2] {'fsdp'}, use_global_device_ids=true, to_apply=%add.1 | all-reduce | flops 6144 | bytes 24576 | tf_op jit(solution)/shard_map/while
  521.0 43.7 %all-gather.11.cloned.1.call-done = bf16[768,2304]{1,0:T(8,128)(2,1)} async-done(((bf16[192,2304]{1,0:T(8,128)(2,1)}), bf16[768,2304]{1,0:T(8,128)(2,1)}) %all-gather.11.cloned.1.call-update) | async-done | bytes 3538960 | tf_op jit(solution)/shard_map/while/body/eval_jaxpr/all_gather | solution.py:114
  564.6 4.1 convolution_bitcast_fusion.2
  569.1 2.8 collective-permute-start
  575.1 13.2 all-gather.3
  596.9 15.3 %fusion.201 = (f32[12,512]{1,0:T(8,128)S(1)}, f32[12,512,1024]{2,1,0:T(8,128)}) fusion(pred[512,1024]{1,0:T(8,128)(4,1)} %fusion.200, bf16[512,12,64]{0,2,1:T(8,128)(2,1)} %bitcast.212, bf16[1024,12,64]{0,2,1:T(8,128)(2,1)} %bitcast.210), kind=kOutput, calls=%fused_computation.8.clone.1 | convolution fusion | flops 824174592 | bytes 28073984 | tf_op jit(solution)/shard_map/while/body/eval_jaxpr/sqhd,skhd->shqk/dot_general | solution.py:61
  612.2 11.8 exponential_reduce_fusion.2
  624.0 12.1 convolution_convert_fusion.4
  636.1 2.7 fusion.202
  639.1 46.4 %all-gather.13.cloned.1.call-done = bf16[768,3072]{1,0:T(8,128)(2,1)} async-done(((bf16[192,3072]{1,0:T(8,128)(2,1)}), bf16[768,3072]{1,0:T(8,128)(2,1)}) %all-gather.13.cloned.1.call-update) | async-done | bytes 4718608 | tf_op jit(solution)/shard_map/while/body/eval_jaxpr/all_gather | solution.py:123
  685.5 7.1 fusion.203
  692.7 82.4 %all-gather.15.cloned.1.call-done = bf16[3072,768]{1,0:T(8,128)(2,1)} async-done(((bf16[768,768]{1,0:T(8,128)(2,1)}), bf16[3072,768]{1,0:T(8,128)(2,1)}) %all-gather.15.cloned.1.call-update) | async-done | bytes 4718608 | tf_op jit(solution)/shard_map/while/body/eval_jaxpr/all_gather | solution.py:163
  775.0 9.7 convert_reduce_fusion.13
  784.7 3.0 multiply_reduce_fusion.9
  793.1 13.6 %fusion.204 = f32[12,64,1024]{2,1,0:T(8,128)} fusion(bf16[512,12,64]{0,2,1:T(8,128)(2,1)} %bitcast.208, f32[12,512]{1,0:T(8,128)S(1)} %log_add_fusion.2, f32[12,512,1024]{2,1,0:T(8,128)} %get-tuple-element.914, pred[512,1024]{1,0:T(8,128)(4,1)} %fusion.200), kind=kOutput, calls=%fused_computation.107.clone.1 | convolution fusion | flops 830472192 | bytes 29646848 | tf_op jit(solution)/shard_map/while/body/eval_jaxpr/shqk,sqhd->skhd/dot_general | solution.py:193
  806.7 10.1 fusion.205
  816.8 52.3 %convert_reduce_fusion.16 = (f32[12,64]{1,0:T(8,128)S(1)}, bf16[12,64,512]{2,1,0:T(8,128)(2,1)}) fusion(bf16[1024,12,64]{0,2,1:T(8,128)(2,1)} %bitcast.211, f32[12,512,1024]{2,1,0:T(8,128)} %fusion.205, f32[12,512]{1,0:T(8,128)S(1)} %log_add_fusion.2, f32[12,512,1024]{2,1,0:T(8,128)} %get-tuple-element.914, pred[512,1024]{1,0:T(8,128)(4,1)} %fusion.200), kind=kOutput, calls=%fused_computation.77.clone.1 | convolution fusion | flops 875698432 | bytes 53242880 | tf_op jit(solution)/shard_map/while/body/eval_jaxpr/shqk,skhd->sqhd/dot_general | solution.py:190
  869.1 54.1 %fusion.206 = f32[12,64,1024]{2,1,0:T(8,128)} fusion(bf16[512,12,64]{0,2,1:T(8,128)(2,1)} %bitcast.213, f32[12,512,1024]{2,1,0:T(8,128)} %fusion.205, f32[12,512]{1,0:T(8,128)S(1)} %log_add_fusion.2, f32[12,512,1024]{2,1,0:T(8,128)} %get-tuple-element.914, pred[512,1024]{1,0:T(8,128)(4,1)} %fusion.200), kind=kOutput, calls=%fused_computation.10.clone.1 | convolution fusion | flops 874519552 | bytes 54812672 | tf_op jit(solution)/shard_map/while/body/eval_jaxpr/shqk,sqhd->skhd/dot_general | solution.py:192
  923.2 13.2 select_add_fusion.31
  936.4 2.4 slice.86
  940.1 7.9 select_add_fusion.29
  950.9 9.1 fusion.209
  962.0 2.5 convert_reduce_fusion.15
  965.1 9.5 select_add_fusion.23
  974.7 2.7 fusion.208
  983.1 2.8 convert_element_type.440
  986.0 5.2 convert_element_type.434
  991.2 6.8 convert_element_type.452
  998.0 6.4 convert_element_type.456
  1004.5 11.2 reduce-scatter.7.cloned.1.call-done
  1015.7 67.2 %reduce-scatter.5.cloned.1.call-done = bf16[192,2304]{1,0:T(8,128)(2,1)} async-done(((bf16[768,2304]{1,0:T(8,128)(2,1)}), bf16[192,2304]{1,0:T(8,128)(2,1)}) %reduce-scatter.5.cloned.1.call-update) | async-done | bytes 884752 | tf_op jit(solution)/shard_map/reduce_scatter | solution.py:231
  1082.9 87.5 %reduce-scatter.9.cloned.1.call-done = bf16[192,3072]{1,0:T(8,128)(2,1)} async-done(((bf16[768,3072]{1,0:T(8,128)(2,1)}), bf16[192,3072]{1,0:T(8,128)(2,1)}) %reduce-scatter.9.cloned.1.call-update) | async-done | bytes 1179664 | tf_op jit(solution)/shard_map/reduce_scatter | solution.py:231
  1170.4 88.0 %reduce-scatter.11.cloned.1.call-done = bf16[768,768]{1,0:T(8,128)(2,1)} async-done(((bf16[3072,768]{1,0:T(8,128)(2,1)}), bf16[768,768]{1,0:T(8,128)(2,1)}) %reduce-scatter.11.cloned.1.call-update) | async-done | bytes 1179664 | tf_op jit(solution)/shard_map/reduce_scatter | solution.py:231
  1260.5 18.3 %all-reduce.28 = (bf16[768]{0:T(1024)(128)(2,1)S(1)}, bf16[768]{0:T(1024)(128)(2,1)S(1)}, bf16[768]{0:T(1024)(128)(2,1)S(1)}, bf16[768]{0:T(1024)(128)(2,1)S(1)}...) all-reduce(bf16[768]{0:T(1024)(128)(2,1)S(1)} %convert_element_type, ...), channel_id=3, replica_groups=mesh['rep'=4,'fsdp'=4,'ctx'=2] {'fsdp'}, use_global_device_ids=true, to_apply=%region_24.25.clone | all-reduce | flops 9216 | bytes 36864
  1279.5 12.3 all-reduce.26
  1296.9 40.1 %all-reduce.33.cloned.1.call-done = (bf16[192,2304]{1,0:T(8,128)(2,1)}, bf16[192,768]{1,0:T(8,128)(2,1)}, bf16[192,3072]{1,0:T(8,128)(2,1)}, bf16[768,768]{1,0:T(8,128)(2,1)}) async-done(((bf16[192,2304]{1,0:T(8,128)(2,1)}, bf16[192,768]{1,0:T(8,128)(2,1)}, bf16[192,3072]{1,0:T(8,128)(2,1)}, bf16[768,768]{1,0:T(8,128)(2,1)}), (bf16[192,2304]{1,0:T(8,128)(2,1)}, bf16[192,768]{1,0:T(8,128)(2,1)}, ...) | async-done | bytes 3538960 | tf_op jit(solution)/shard_map/psum | solution.py:234
  1338.8 2.6 convert_element_type.435
  (393 shorter events, 86.1 us)
Async XLA Ops:
  8.6 99.5 %copy-start.21 = (s32[1024]{0:T(1024)}, s32[1024]{0:T(1024)S(1)}, u32[]{:S(2)}) copy-start(s32[1024]{0:T(1024)S(1)} %get-tuple-element.1055) | copy-start | bytes 12292 | tf_op jit(solution)/shard_map/while
  8.6 99.5 %copy-start.41 = (pred[1024]{0:T(1024)(128)(4,1)}, pred[1024]{0:T(1024)(128)(4,1)S(1)}, u32[]{:S(2)}) copy-start(pred[1024]{0:T(1024)(128)(4,1)S(1)} %get-tuple-element.1056) | copy-start | bytes 3076 | tf_op jit(solution)/shard_map/while
  8.7 33.7 %copy-start.4 = (bf16[2,1,512,768]{3,2,1,0:T(8,128)(2,1)S(1)}, bf16[2,1,512,768]{3,2,1,0:T(8,128)(2,1)}, u32[]{:S(2)}) copy-start(bf16[2,1,512,768]{3,2,1,0:T(8,128)(2,1)} %get-tuple-element.1040) | copy-start | bytes 4718596 | tf_op jit(solution)/shard_map/while
  8.7 75.6 %all-gather.11.cloned.1.call-start = ((), (), s32[]{:S(2)}) async-start(), calls=%async_computation.10 | async-start | bytes 4423680 | tf_op jit(solution)/shard_map/while/body/eval_jaxpr/all_gather | solution.py:114
  9.4 146.5 %all-gather.9.cloned.1.call-start = ((), (), s32[]{:S(2)}) async-start(), calls=%async_computation.9 | async-start | bytes 1474560 | tf_op jit(solution)/shard_map/while/body/eval_jaxpr/all_gather | solution.py:117
  10.2 195.0 %all-gather.13.cloned.1.call-start = ((), (), s32[]{:S(2)}) async-start(), calls=%async_computation.11 | async-start | bytes 5898240 | tf_op jit(solution)/shard_map/while/body/eval_jaxpr/all_gather | solution.py:123
  10.9 283.6 %all-gather.15.cloned.1.call-start = ((), (), s32[]{:S(2)}) async-start(), calls=%async_computation.12 | async-start | bytes 5898240 | tf_op jit(solution)/shard_map/while/body/eval_jaxpr/all_gather | solution.py:163
  88.4 6.2 copy-start.40
  88.5 19.5 %copy-start.12 = (bf16[2,1,512,768]{3,2,1,0:T(8,128)(2,1)S(1)}, bf16[2,1,512,768]{3,2,1,0:T(8,128)(2,1)}, u32[]{:S(2)}) copy-start(bf16[2,1,512,768]{3,2,1,0:T(8,128)(2,1)} %get-tuple-element.1045) | copy-start | bytes 4718596 | tf_op jit(solution)/shard_map/while
  88.8 21.7 %collective-permute-start = (bf16[1,512,768]{2,1,0:T(8,128)(2,1)S(1)}, bf16[1,512,768]{2,1,0:T(8,128)(2,1)}, u32[]{:S(2)}, u32[]{:S(2)}) collective-permute-start(bf16[1,512,768]{2,1,0:T(8,128)(2,1)S(1)} %get-tuple-element.911), channel_id=1, source_target_pairs={{0,1},{2,3},{4,5},{6,7},{8,9},{10,11},{12,13},{14,15},{16,17},{18,... | collective-permute-start | bytes 2359304 | tf_op jit(solution)/shard_map/while/body/eval_jaxpr/ppermute | solution.py:14
  92.5 20.6 %collective-permute-start.1 = (bf16[1,512,768]{2,1,0:T(8,128)(2,1)}, bf16[1,512,768]{2,1,0:T(8,128)(2,1)}, u32[]{:S(2)}, u32[]{:S(2)}) collective-permute-start(bf16[1,512,768]{2,1,0:T(8,128)(2,1)} %slice.85), channel_id=1, source_target_pairs={{0,1},{2,3},{4,5},{6,7},{8,9},{10,11},{12,13},{14,15},{16,17},{18,... | collective-permute-start | bytes 2359304 | tf_op jit(solution)/shard_map/while/body/eval_jaxpr/ppermute | solution.py:14
  108.1 4.9 copy-start.23
  113.0 30.8 %copy-start = (bf16[1,1024,768]{1,2,0:T(8,128)(2,1)}, bf16[1,1024,768]{1,2,0:T(8,128)(2,1)S(1)}, u32[]{:S(2)}) copy-start(bf16[1,1024,768]{1,2,0:T(8,128)(2,1)S(1)} %copy.50) | copy-start | bytes 4718596 | tf_op jit(solution)/shard_map/while
  116.7 15.2 %copy-start.3 = (pred[512,1024]{1,0:T(8,128)(4,1)S(1)}, pred[512,1024]{1,0:T(8,128)(4,1)}, u32[]{:S(2)}) copy-start(pred[512,1024]{1,0:T(8,128)(4,1)} %fusion.200) | copy-start | bytes 1572868 | tf_op jit(solution)/shard_map/while
  158.9 135.6 %copy-start.13 = (bf16[2,1,512,768]{3,2,1,0:T(8,128)(2,1)S(1)}, bf16[2,1,512,768]{3,2,1,0:T(8,128)(2,1)}, u32[]{:S(2)}) copy-start(bf16[2,1,512,768]{3,2,1,0:T(8,128)(2,1)} %get-tuple-element.1045) | copy-start | bytes 4718596 | tf_op jit(solution)/shard_map/while
  294.5 9.3 copy-start.43
  312.2 13.6 %copy-start.1 = (bf16[1,1024,768]{1,2,0:T(8,128)(2,1)S(1)}, bf16[1,1024,768]{1,2,0:T(8,128)(2,1)}, u32[]{:S(2)}) copy-start(bf16[1,1024,768]{1,2,0:T(8,128)(2,1)} %copy-done) | copy-start | bytes 4718596 | tf_op jit(solution)/shard_map/while
  312.2 13.6 %copy-start.2 = (bf16[512,768]{0,1:T(8,128)(2,1)S(1)}, bf16[512,768]{0,1:T(8,128)(2,1)}, u32[]{:S(2)}) copy-start(bf16[512,768]{0,1:T(8,128)(2,1)} %copy.53) | copy-start | bytes 2359300 | tf_op jit(solution)/shard_map/while
  442.5 14.2 %copy-start.9 = (bf16[512,3072]{1,0:T(8,128)(2,1)S(1)}, bf16[512,3072]{1,0:T(8,128)(2,1)}, u32[]{:S(2)}) copy-start(bf16[512,3072]{1,0:T(8,128)(2,1)} %copy-done.8) | copy-start | bytes 9437188 | tf_op jit(solution)/shard_map/while
  455.4 20.5 %collective-permute-start.2 = (bf16[1,512,768]{1,2,0:T(8,128)(2,1)}, bf16[1,512,768]{1,2,0:T(8,128)(2,1)}, u32[]{:S(2)}, u32[]{:S(2)}) collective-permute-start(bf16[1,512,768]{1,2,0:T(8,128)(2,1)} %slice.86), channel_id=1, source_target_pairs={{1,0},{3,2},{5,4},{7,6},{9,8},{11,10},{13,12},{15,14},{17,16},{19,... | collective-permute-start | bytes 2359304 | tf_op jit(solution)/shard_map/while/body/eval_jaxpr/ppermute | solution.py:14
  463.9 14.9 %collective-permute-start.3 = (bf16[1,512,768]{1,2,0:T(8,128)(2,1)S(1)}, bf16[1,512,768]{1,2,0:T(8,128)(2,1)S(1)}, u32[]{:S(2)}, u32[]{:S(2)}) collective-permute-start(bf16[1,512,768]{1,2,0:T(8,128)(2,1)S(1)} %slice.87), channel_id=1, source_target_pairs={{1,0},{3,2},{5,4},{7,6},{9,8},{11,10},{13,12},{15,14},{17,16},{19,... | collective-permute-start | bytes 2359304 | tf_op jit(solution)/shard_map/while/body/eval_jaxpr/ppermute | solution.py:14
  465.2 9.2 copy-start.6
  465.2 9.2 copy-start.15
  478.8 7.9 copy-start.35
  479.5 7.3 copy-start.44
  492.0 96.5 %copy-start.21 = (s32[1024]{0:T(1024)}, s32[1024]{0:T(1024)S(1)}, u32[]{:S(2)}) copy-start(s32[1024]{0:T(1024)S(1)} %get-tuple-element.1055) | copy-start | bytes 12292 | tf_op jit(solution)/shard_map/while
  492.0 96.5 %copy-start.41 = (pred[1024]{0:T(1024)(128)(4,1)}, pred[1024]{0:T(1024)(128)(4,1)S(1)}, u32[]{:S(2)}) copy-start(pred[1024]{0:T(1024)(128)(4,1)S(1)} %get-tuple-element.1056) | copy-start | bytes 3076 | tf_op jit(solution)/shard_map/while
  492.0 28.5 %copy-start.4 = (bf16[2,1,512,768]{3,2,1,0:T(8,128)(2,1)S(1)}, bf16[2,1,512,768]{3,2,1,0:T(8,128)(2,1)}, u32[]{:S(2)}) copy-start(bf16[2,1,512,768]{3,2,1,0:T(8,128)(2,1)} %get-tuple-element.1040) | copy-start | bytes 4718596 | tf_op jit(solution)/shard_map/while
  492.1 72.5 %all-gather.11.cloned.1.call-start = ((), (), s32[]{:S(2)}) async-start(), calls=%async_computation.10 | async-start | bytes 4423680 | tf_op jit(solution)/shard_map/while/body/eval_jaxpr/all_gather | solution.py:114
  492.7 143.5 %all-gather.9.cloned.1.call-start = ((), (), s32[]{:S(2)}) async-start(), calls=%async_computation.9 | async-start | bytes 1474560 | tf_op jit(solution)/shard_map/while/body/eval_jaxpr/all_gather | solution.py:117
  493.2 192.3 %all-gather.13.cloned.1.call-start = ((), (), s32[]{:S(2)}) async-start(), calls=%async_computation.11 | async-start | bytes 5898240 | tf_op jit(solution)/shard_map/while/body/eval_jaxpr/all_gather | solution.py:123
  494.0 281.0 %all-gather.15.cloned.1.call-start = ((), (), s32[]{:S(2)}) async-start(), calls=%async_computation.12 | async-start | bytes 5898240 | tf_op jit(solution)/shard_map/while/body/eval_jaxpr/all_gather | solution.py:163
  568.8 6.3 copy-start.40
  568.8 19.6 %copy-start.12 = (bf16[2,1,512,768]{3,2,1,0:T(8,128)(2,1)S(1)}, bf16[2,1,512,768]{3,2,1,0:T(8,128)(2,1)}, u32[]{:S(2)}) copy-start(bf16[2,1,512,768]{3,2,1,0:T(8,128)(2,1)} %get-tuple-element.1045) | copy-start | bytes 4718596 | tf_op jit(solution)/shard_map/while
  569.1 21.8 %collective-permute-start = (bf16[1,512,768]{2,1,0:T(8,128)(2,1)S(1)}, bf16[1,512,768]{2,1,0:T(8,128)(2,1)}, u32[]{:S(2)}, u32[]{:S(2)}) collective-permute-start(bf16[1,512,768]{2,1,0:T(8,128)(2,1)S(1)} %get-tuple-element.911), channel_id=1, source_target_pairs={{0,1},{2,3},{4,5},{6,7},{8,9},{10,11},{12,13},{14,15},{16,17},{18,... | collective-permute-start | bytes 2359304 | tf_op jit(solution)/shard_map/while/body/eval_jaxpr/ppermute | solution.py:14
  572.9 20.3 %collective-permute-start.1 = (bf16[1,512,768]{2,1,0:T(8,128)(2,1)}, bf16[1,512,768]{2,1,0:T(8,128)(2,1)}, u32[]{:S(2)}, u32[]{:S(2)}) collective-permute-start(bf16[1,512,768]{2,1,0:T(8,128)(2,1)} %slice.85), channel_id=1, source_target_pairs={{0,1},{2,3},{4,5},{6,7},{8,9},{10,11},{12,13},{14,15},{16,17},{18,... | collective-permute-start | bytes 2359304 | tf_op jit(solution)/shard_map/while/body/eval_jaxpr/ppermute | solution.py:14
  588.5 4.7 copy-start.23
  593.2 30.8 %copy-start = (bf16[1,1024,768]{1,2,0:T(8,128)(2,1)}, bf16[1,1024,768]{1,2,0:T(8,128)(2,1)S(1)}, u32[]{:S(2)}) copy-start(bf16[1,1024,768]{1,2,0:T(8,128)(2,1)S(1)} %copy.50) | copy-start | bytes 4718596 | tf_op jit(solution)/shard_map/while
  596.9 15.3 %copy-start.3 = (pred[512,1024]{1,0:T(8,128)(4,1)S(1)}, pred[512,1024]{1,0:T(8,128)(4,1)}, u32[]{:S(2)}) copy-start(pred[512,1024]{1,0:T(8,128)(4,1)} %fusion.200) | copy-start | bytes 1572868 | tf_op jit(solution)/shard_map/while
  639.1 135.9 %copy-start.13 = (bf16[2,1,512,768]{3,2,1,0:T(8,128)(2,1)S(1)}, bf16[2,1,512,768]{3,2,1,0:T(8,128)(2,1)}, u32[]{:S(2)}) copy-start(bf16[2,1,512,768]{3,2,1,0:T(8,128)(2,1)} %get-tuple-element.1045) | copy-start | bytes 4718596 | tf_op jit(solution)/shard_map/while
  775.0 9.7 copy-start.43
  793.1 13.6 %copy-start.1 = (bf16[1,1024,768]{1,2,0:T(8,128)(2,1)S(1)}, bf16[1,1024,768]{1,2,0:T(8,128)(2,1)}, u32[]{:S(2)}) copy-start(bf16[1,1024,768]{1,2,0:T(8,128)(2,1)} %copy-done) | copy-start | bytes 4718596 | tf_op jit(solution)/shard_map/while
  793.1 13.6 %copy-start.2 = (bf16[512,768]{0,1:T(8,128)(2,1)S(1)}, bf16[512,768]{0,1:T(8,128)(2,1)}, u32[]{:S(2)}) copy-start(bf16[512,768]{0,1:T(8,128)(2,1)} %copy.53) | copy-start | bytes 2359300 | tf_op jit(solution)/shard_map/while
  923.2 16.9 %copy-start.9 = (bf16[512,3072]{1,0:T(8,128)(2,1)S(1)}, bf16[512,3072]{1,0:T(8,128)(2,1)}, u32[]{:S(2)}) copy-start(bf16[512,3072]{1,0:T(8,128)(2,1)} %copy-done.8) | copy-start | bytes 9437188 | tf_op jit(solution)/shard_map/while
  938.8 22.8 %collective-permute-start.2 = (bf16[1,512,768]{1,2,0:T(8,128)(2,1)}, bf16[1,512,768]{1,2,0:T(8,128)(2,1)}, u32[]{:S(2)}, u32[]{:S(2)}) collective-permute-start(bf16[1,512,768]{1,2,0:T(8,128)(2,1)} %slice.86), channel_id=1, source_target_pairs={{1,0},{3,2},{5,4},{7,6},{9,8},{11,10},{13,12},{15,14},{17,16},{19,... | collective-permute-start | bytes 2359304 | tf_op jit(solution)/shard_map/while/body/eval_jaxpr/ppermute | solution.py:14
  949.6 15.0 %collective-permute-start.3 = (bf16[1,512,768]{1,2,0:T(8,128)(2,1)S(1)}, bf16[1,512,768]{1,2,0:T(8,128)(2,1)S(1)}, u32[]{:S(2)}, u32[]{:S(2)}) collective-permute-start(bf16[1,512,768]{1,2,0:T(8,128)(2,1)S(1)} %slice.87), channel_id=1, source_target_pairs={{1,0},{3,2},{5,4},{7,6},{9,8},{11,10},{13,12},{15,14},{17,16},{19,... | collective-permute-start | bytes 2359304 | tf_op jit(solution)/shard_map/while/body/eval_jaxpr/ppermute | solution.py:14
  950.9 9.2 copy-start.6
  950.9 9.2 copy-start.15
  964.5 10.1 copy-start.35
  965.1 9.5 copy-start.44
  983.0 32.7 %reduce-scatter.7.cloned.1.call-start = ((), (), s32[]{:S(2)}) async-start(), calls=%async_computation.5 | async-start | bytes 1474560 | tf_op jit(solution)/shard_map/reduce_scatter | solution.py:231
  985.9 97.0 %reduce-scatter.5.cloned.1.call-start = ((), (), s32[]{:S(2)}) async-start(), calls=%async_computation.4 | async-start | bytes 4423680 | tf_op jit(solution)/shard_map/reduce_scatter | solution.py:231
  991.1 179.3 %reduce-scatter.9.cloned.1.call-start = ((), (), s32[]{:S(2)}) async-start(), calls=%async_computation.6 | async-start | bytes 5898240 | tf_op jit(solution)/shard_map/reduce_scatter | solution.py:231
  998.0 260.5 %reduce-scatter.11.cloned.1.call-start = ((), (), s32[]{:S(2)}) async-start(), calls=%async_computation.7 | async-start | bytes 5898240 | tf_op jit(solution)/shard_map/reduce_scatter | solution.py:231
  1004.4 254.1 %copy-start.49 = (u32[32]{0:T(128)S(1)}, u32[32]{0:T(128)}, u32[]{:S(2)}) copy-start(u32[32]{0:T(128)} %get-tuple-element.1116) | copy-start | bytes 388
  1004.4 256.0 %copy-start.39 = (f32[768]{0:T(1024)S(1)}, f32[768]{0:T(1024)}, u32[]{:S(2)}) copy-start(f32[768]{0:T(1024)} %get-tuple-element.421) | copy-start | bytes 9220
  1004.4 256.0 %copy-start.36 = (f32[768]{0:T(1024)S(1)}, f32[768]{0:T(1024)}, u32[]{:S(2)}) copy-start(f32[768]{0:T(1024)} %get-tuple-element.422) | copy-start | bytes 9220
  1004.4 256.0 %copy-start.33 = (f32[768]{0:T(1024)S(1)}, f32[768]{0:T(1024)}, u32[]{:S(2)}) copy-start(f32[768]{0:T(1024)} %get-tuple-element.424) | copy-start | bytes 9220
  1004.4 256.0 %copy-start.30 = (f32[768]{0:T(1024)S(1)}, f32[768]{0:T(1024)}, u32[]{:S(2)}) copy-start(f32[768]{0:T(1024)} %get-tuple-element.425) | copy-start | bytes 9220
  1004.4 256.1 %copy-start.27 = (f32[768]{0:T(1024)S(1)}, f32[768]{0:T(1024)}, u32[]{:S(2)}) copy-start(f32[768]{0:T(1024)} %get-tuple-element.426) | copy-start | bytes 9220
  1004.4 256.1 %copy-start.20 = (f32[3072]{0:T(1024)S(1)}, f32[3072]{0:T(1024)}, u32[]{:S(2)}) copy-start(f32[3072]{0:T(1024)} %get-tuple-element.430) | copy-start | bytes 36868
  1004.5 332.5 %all-reduce.33.cloned.1.call-start = ((), (), s32[]{:S(2)}) async-start(), calls=%async_computation.8 | async-start | bytes 7077888 | tf_op jit(solution)/shard_map/psum | solution.py:234
  1336.9 4.5 copy-start.17
  1338.8 4.3 copy-start.16
  (48 other events, 117.0 us)
Sparse Core Ops, SparseCore 0:
  11.1 73.1 all-gather.10
  85.9 29.1 all-gather.8
  116.6 88.5 all-gather.12
  206.6 87.8 all-gather.14
  494.2 70.3 all-gather.10
  566.0 29.3 all-gather.8
  597.0 88.5 all-gather.12
  687.1 87.8 all-gather.14
Sparse Core Ops, SparseCore 1:
  986.4 29.2 reduce-scatter.6
  1017.9 65.0 reduce-scatter.4
  1085.1 85.3 reduce-scatter.8
  1172.8 85.6 reduce-scatter.10
  1262.2 74.7 all-reduce.32
where the time goes:
time: 1360 us; the launch traced here: 1350 us
  waiting for transfers between devices  640 us (47%)
  matrix products  452 us (33%)
  blocking collectives  94.9 us (7%)
  other arithmetic  79.7 us (6%)
  local copies, waits for them, and re-layouts  45.7 us (3%)
  between operations  17.5 us (1%)
  starting transfers between devices  15.6 us (1%)
    reduce_scatter x4, waiting for transfers between devices, local(): lax.psum_scatter(for_sending(totals), 'fsdp', scatter_dimension=0, tiled=...  254 us
    all_gather x2, waiting for transfers between devices, micro(): lax.all_gather(shards[11], 'fsdp', axis=0, tiled=True)  165 us
    dot_general x2, matrix products, micro(): jnp.einsum('shqk,sqhd->skhd', d_scores, query_heads, preferred_element_ty...  108 us
    dot_general x2, matrix products, micro(): jnp.einsum('shqk,skhd->sqhd', d_scores, key_heads, preferred_element_type...  105 us
    all_gather x2, waiting for transfers between devices, micro(): lax.all_gather(shards[9], 'fsdp', axis=0, tiled=True)  92.7 us
    all_gather x2, waiting for transfers between devices, micro(): lax.all_gather(shards[0], 'fsdp', axis=0, tiled=True)  85.2 us
    dot_general x8, matrix products, outer_sum(): jnp.einsum('sri,srj->ij', left, right, preferred_element_type=jnp.float32)  56.7 us
    dot_general x8, matrix products, project(): jnp.einsum('sri,ij->srj', left, weight, preferred_element_type=jnp.float32)  46.1 us
  transfers between devices with their start and end apart: 21, of which 11 were waited for; matrix products, arithmetic and copies ran while one was open for 16% of the time, Pallas kernels for 0%

commit v1 on v0

--- a/solution.py
+++ b/solution.py
@@ -230,8 +230,14 @@
         lambda part: part.astype(jnp.float32),
         lax.psum_scatter(for_sending(totals), "fsdp", scatter_dimension=0, tiled=True),
     )
+
+    def _attach_positions(mine):
+        for j in ("ctx", "rep"):
+            mine = lax.psum(mine, j)
+        return mine
+
     summed = jax.tree.map(
-        lambda part: part.astype(jnp.float32), lax.psum(for_sending(shares), ("rep", "ctx"))
+        lambda part: part.astype(jnp.float32), _attach_positions(for_sending(shares))
     )
     return (results, grad_tokens) + tuple(summed)
 

time: 1360 us -> 1400 us (1.029)
  waiting for transfers between devices: 640 us -> 687 us
    psum x1 -> x2, waiting for transfers between devices: 40.1 us -> 86.4 us  [_attach_positions(): mine = lax.psum(mine, j)]
  transfers between devices with their start and end apart: 21 -> 22, of which waited for: 11 -> 12; matrix products, arithmetic and copies ran while one was open for 16% -> 15% of each run, Pallas kernels for 0% -> 0%
where the time goes in v1:
time: 1400 us
  waiting for transfers between devices  687 us (49%)
  matrix products  452 us (32%)
  blocking collectives  96.5 us (7%)
  other arithmetic  79.7 us (6%)
  local copies, waits for them, and re-layouts  45.7 us (3%)
  between operations  17.4 us (1%)
  starting transfers between devices  15.5 us (1%)
    reduce_scatter x4, waiting for transfers between devices, local(): lax.psum_scatter(for_sending(totals), 'fsdp', scatter_dimension=0, tiled=...  254 us
    all_gather x2, waiting for transfers between devices, micro(): lax.all_gather(shards[11], 'fsdp', axis=0, tiled=True)  165 us
    dot_general x2, matrix products, micro(): jnp.einsum('shqk,sqhd->skhd', d_scores, query_heads, preferred_element_ty...  108 us
    dot_general x2, matrix products, micro(): jnp.einsum('shqk,skhd->sqhd', d_scores, key_heads, preferred_element_type...  105 us
    all_gather x2, waiting for transfers between devices, micro(): lax.all_gather(shards[9], 'fsdp', axis=0, tiled=True)  93.1 us
    psum x2, waiting for transfers between devices, _attach_positions(): mine = lax.psum(mine, j)  86.4 us
    all_gather x2, waiting for transfers between devices, micro(): lax.all_gather(shards[0], 'fsdp', axis=0, tiled=True)  85.2 us
    dot_general x8, matrix products, outer_sum(): jnp.einsum('sri,srj->ij', left, right, preferred_element_type=jnp.float32)  56.8 us
  transfers between devices with their start and end apart: 22, of which 12 were waited for; matrix products, arithmetic and copies ran while one was open for 15% of the time, Pallas kernels for 0%

profile of v1, /device:TPU:0, one launch (start us, length us, event | category | flops | bytes accessed | tf_op | source)
XLA Modules:
  0.0 1401.1 jit_solution(9024046655045988966)
XLA Ops:
  8.2 975.7 %while.41 = (s32[]{:T(128)}, f32[768,2304]{1,0:T(8,128)}, f32[768]{0:T(1024)}, f32[768]{0:T(1024)}, f32[768,768]{1,0:T(8,128)}, /*index=5*/f32[768]{0:T(1024)}, ...) while((s32[]{:T(128)}, f32[768,2304]{1,0:T(8,128)}, ...), condition=%wide.region_21.22_spmd.clone, body=%wide.region_0.21_spmd.clone.sunk | while | flops 26950144000 | bytes 699213696 | solution.py:228
  19.6 21.5 %all-reduce.32 = (bf16[768]{0:T(1024)(128)(2,1)S(1)}, bf16[768]{0:T(1024)(128)(2,1)S(1)}, bf16[768]{0:T(1024)(128)(2,1)S(1)}, bf16[768]{0:T(1024)(128)(2,1)S(1)}...) all-reduce(bf16[768]{0:T(1024)(128)(2,1)S(1)} %dynamic-update-slice, ...), channel_id=1, replica_groups=mesh['rep'=4,'fsdp'=4,'ctx'=2] {'fsdp'}, use_global_device_ids=true, to_apply=%add.1 | all-reduce | flops 6144 | bytes 24576 | tf_op jit(solution)/shard_map/while
  42.8 41.6 %all-gather.11.cloned.1.call-done = bf16[768,2304]{1,0:T(8,128)(2,1)} async-done(((bf16[192,2304]{1,0:T(8,128)(2,1)}), bf16[768,2304]{1,0:T(8,128)(2,1)}) %all-gather.11.cloned.1.call-update) | async-done | bytes 3538960 | tf_op jit(solution)/shard_map/while/body/eval_jaxpr/all_gather | solution.py:114
  84.4 4.2 convolution_bitcast_fusion.2
  88.9 2.7 collective-permute-start
  94.8 13.2 all-gather.3
  116.8 15.3 %fusion.201 = (f32[12,512]{1,0:T(8,128)S(1)}, f32[12,512,1024]{2,1,0:T(8,128)}) fusion(pred[512,1024]{1,0:T(8,128)(4,1)} %fusion.200, bf16[512,12,64]{0,2,1:T(8,128)(2,1)} %bitcast.212, bf16[1024,12,64]{0,2,1:T(8,128)(2,1)} %bitcast.210), kind=kOutput, calls=%fused_computation.8.clone.1 | convolution fusion | flops 824174592 | bytes 28073984 | tf_op jit(solution)/shard_map/while/body/eval_jaxpr/sqhd,skhd->shqk/dot_general | solution.py:61
  132.0 11.8 exponential_reduce_fusion.2
  143.9 12.1 convolution_convert_fusion.4
  156.0 2.7 fusion.202
  159.0 46.4 %all-gather.13.cloned.1.call-done = bf16[768,3072]{1,0:T(8,128)(2,1)} async-done(((bf16[192,3072]{1,0:T(8,128)(2,1)}), bf16[768,3072]{1,0:T(8,128)(2,1)}) %all-gather.13.cloned.1.call-update) | async-done | bytes 4718608 | tf_op jit(solution)/shard_map/while/body/eval_jaxpr/all_gather | solution.py:123
  205.4 7.1 fusion.203
  212.5 82.3 %all-gather.15.cloned.1.call-done = bf16[3072,768]{1,0:T(8,128)(2,1)} async-done(((bf16[768,768]{1,0:T(8,128)(2,1)}), bf16[3072,768]{1,0:T(8,128)(2,1)}) %all-gather.15.cloned.1.call-update) | async-done | bytes 4718608 | tf_op jit(solution)/shard_map/while/body/eval_jaxpr/all_gather | solution.py:163
  294.8 9.3 convert_reduce_fusion.13
  304.2 3.0 multiply_reduce_fusion.9
  312.5 13.6 fusion.204
  326.2 10.1 fusion.205
  336.2 52.4 %convert_reduce_fusion.16 = (f32[12,64]{1,0:T(8,128)S(1)}, bf16[12,64,512]{2,1,0:T(8,128)(2,1)}) fusion(bf16[1024,12,64]{0,2,1:T(8,128)(2,1)} %bitcast.211, f32[12,512,1024]{2,1,0:T(8,128)} %fusion.205, f32[12,512]{1,0:T(8,128)S(1)} %log_add_fusion.2, f32[12,512,1024]{2,1,0:T(8,128)} %get-tuple-element.927, pred[512,1024]{1,0:T(8,128)(4,1)} %fusion.200), kind=kOutput, calls=%fused_computation.77.clone.1 | convolution fusion | flops 875698432 | bytes 53242880 | tf_op jit(solution)/shard_map/while/body/eval_jaxpr/shqk,skhd->sqhd/dot_general | solution.py:190
  388.6 54.2 %fusion.206 = f32[12,64,1024]{2,1,0:T(8,128)} fusion(bf16[512,12,64]{0,2,1:T(8,128)(2,1)} %bitcast.213, f32[12,512,1024]{2,1,0:T(8,128)} %fusion.205, f32[12,512]{1,0:T(8,128)S(1)} %log_add_fusion.2, f32[12,512,1024]{2,1,0:T(8,128)} %get-tuple-element.927, pred[512,1024]{1,0:T(8,128)(4,1)} %fusion.200), kind=kOutput, calls=%fused_computation.10.clone.1 | convolution fusion | flops 874519552 | bytes 54812672 | tf_op jit(solution)/shard_map/while/body/eval_jaxpr/shqk,sqhd->skhd/dot_general | solution.py:192
  442.8 10.5 select_add_fusion.31
  457.0 5.6 select_add_fusion.29
  465.6 9.1 fusion.209
  476.6 2.5 convert_reduce_fusion.15
  479.8 7.3 select_add_fusion.23
  487.1 2.7 fusion.208
  503.0 16.6 %all-reduce.32 = (bf16[768]{0:T(1024)(128)(2,1)S(1)}, bf16[768]{0:T(1024)(128)(2,1)S(1)}, bf16[768]{0:T(1024)(128)(2,1)S(1)}, bf16[768]{0:T(1024)(128)(2,1)S(1)}...) all-reduce(bf16[768]{0:T(1024)(128)(2,1)S(1)} %dynamic-update-slice, ...), channel_id=1, replica_groups=mesh['rep'=4,'fsdp'=4,'ctx'=2] {'fsdp'}, use_global_device_ids=true, to_apply=%add.1 | all-reduce | flops 6144 | bytes 24576 | tf_op jit(solution)/shard_map/while
  521.3 43.7 %all-gather.11.cloned.1.call-done = bf16[768,2304]{1,0:T(8,128)(2,1)} async-done(((bf16[192,2304]{1,0:T(8,128)(2,1)}), bf16[768,2304]{1,0:T(8,128)(2,1)}) %all-gather.11.cloned.1.call-update) | async-done | bytes 3538960 | tf_op jit(solution)/shard_map/while/body/eval_jaxpr/all_gather | solution.py:114
  565.0 4.2 convolution_bitcast_fusion.2
  569.5 2.7 collective-permute-start
  575.5 13.2 all-gather.3
  597.2 15.3 %fusion.201 = (f32[12,512]{1,0:T(8,128)S(1)}, f32[12,512,1024]{2,1,0:T(8,128)}) fusion(pred[512,1024]{1,0:T(8,128)(4,1)} %fusion.200, bf16[512,12,64]{0,2,1:T(8,128)(2,1)} %bitcast.212, bf16[1024,12,64]{0,2,1:T(8,128)(2,1)} %bitcast.210), kind=kOutput, calls=%fused_computation.8.clone.1 | convolution fusion | flops 824174592 | bytes 28073984 | tf_op jit(solution)/shard_map/while/body/eval_jaxpr/sqhd,skhd->shqk/dot_general | solution.py:61
  612.5 11.8 exponential_reduce_fusion.2
  624.4 12.1 convolution_convert_fusion.4
  636.5 2.7 fusion.202
  639.5 46.7 %all-gather.13.cloned.1.call-done = bf16[768,3072]{1,0:T(8,128)(2,1)} async-done(((bf16[192,3072]{1,0:T(8,128)(2,1)}), bf16[768,3072]{1,0:T(8,128)(2,1)}) %all-gather.13.cloned.1.call-update) | async-done | bytes 4718608 | tf_op jit(solution)/shard_map/while/body/eval_jaxpr/all_gather | solution.py:123
  686.2 7.1 fusion.203
  693.3 82.5 %all-gather.15.cloned.1.call-done = bf16[3072,768]{1,0:T(8,128)(2,1)} async-done(((bf16[768,768]{1,0:T(8,128)(2,1)}), bf16[3072,768]{1,0:T(8,128)(2,1)}) %all-gather.15.cloned.1.call-update) | async-done | bytes 4718608 | tf_op jit(solution)/shard_map/while/body/eval_jaxpr/all_gather | solution.py:163
  775.7 9.7 convert_reduce_fusion.13
  785.4 3.0 multiply_reduce_fusion.9
  793.8 13.6 fusion.204
  807.4 10.1 fusion.205
  817.5 52.3 %convert_reduce_fusion.16 = (f32[12,64]{1,0:T(8,128)S(1)}, bf16[12,64,512]{2,1,0:T(8,128)(2,1)}) fusion(bf16[1024,12,64]{0,2,1:T(8,128)(2,1)} %bitcast.211, f32[12,512,1024]{2,1,0:T(8,128)} %fusion.205, f32[12,512]{1,0:T(8,128)S(1)} %log_add_fusion.2, f32[12,512,1024]{2,1,0:T(8,128)} %get-tuple-element.927, pred[512,1024]{1,0:T(8,128)(4,1)} %fusion.200), kind=kOutput, calls=%fused_computation.77.clone.1 | convolution fusion | flops 875698432 | bytes 53242880 | tf_op jit(solution)/shard_map/while/body/eval_jaxpr/shqk,skhd->sqhd/dot_general | solution.py:190
  869.8 54.0 %fusion.206 = f32[12,64,1024]{2,1,0:T(8,128)} fusion(bf16[512,12,64]{0,2,1:T(8,128)(2,1)} %bitcast.213, f32[12,512,1024]{2,1,0:T(8,128)} %fusion.205, f32[12,512]{1,0:T(8,128)S(1)} %log_add_fusion.2, f32[12,512,1024]{2,1,0:T(8,128)} %get-tuple-element.927, pred[512,1024]{1,0:T(8,128)(4,1)} %fusion.200), kind=kOutput, calls=%fused_computation.10.clone.1 | convolution fusion | flops 874519552 | bytes 54812672 | tf_op jit(solution)/shard_map/while/body/eval_jaxpr/shqk,sqhd->skhd/dot_general | solution.py:192
  923.9 13.3 select_add_fusion.31
  937.2 2.4 slice.86
  940.9 7.9 select_add_fusion.29
  951.7 9.1 fusion.209
  962.7 2.5 convert_reduce_fusion.15
  965.9 9.5 select_add_fusion.23
  975.4 2.7 fusion.208
  983.9 2.8 convert_element_type.440
  986.8 5.2 convert_element_type.434
  992.1 6.8 convert_element_type.452
  998.9 6.4 convert_element_type.456
  1005.3 11.2 reduce-scatter.7.cloned.1.call-done
  1016.6 67.2 %reduce-scatter.5.cloned.1.call-done = bf16[192,2304]{1,0:T(8,128)(2,1)} async-done(((bf16[768,2304]{1,0:T(8,128)(2,1)}), bf16[192,2304]{1,0:T(8,128)(2,1)}) %reduce-scatter.5.cloned.1.call-update) | async-done | bytes 884752 | tf_op jit(solution)/shard_map/reduce_scatter | solution.py:231
  1083.8 87.5 %reduce-scatter.9.cloned.1.call-done = bf16[192,3072]{1,0:T(8,128)(2,1)} async-done(((bf16[768,3072]{1,0:T(8,128)(2,1)}), bf16[192,3072]{1,0:T(8,128)(2,1)}) %reduce-scatter.9.cloned.1.call-update) | async-done | bytes 1179664 | tf_op jit(solution)/shard_map/reduce_scatter | solution.py:231
  1171.3 88.0 %reduce-scatter.11.cloned.1.call-done = bf16[768,768]{1,0:T(8,128)(2,1)} async-done(((bf16[3072,768]{1,0:T(8,128)(2,1)}), bf16[768,768]{1,0:T(8,128)(2,1)}) %reduce-scatter.11.cloned.1.call-update) | async-done | bytes 1179664 | tf_op jit(solution)/shard_map/reduce_scatter | solution.py:231
  1259.4 26.9 %all-reduce.38.cloned.1.call-done = (bf16[192,2304]{1,0:T(8,128)(2,1)}, bf16[192,768]{1,0:T(8,128)(2,1)}, bf16[192,3072]{1,0:T(8,128)(2,1)}, bf16[768,768]{1,0:T(8,128)(2,1)}) async-done(((bf16[192,2304]{1,0:T(8,128)(2,1)}, bf16[192,768]{1,0:T(8,128)(2,1)}, bf16[192,3072]{1,0:T(8,128)(2,1)}, bf16[768,768]{1,0:T(8,128)(2,1)}), (bf16[192,2304]{1,0:T(8,128)(2,1)}, bf16[192,768]{1,0:T(8,128)(2,1)}, ...) | async-done | bytes 3538960 | tf_op jit(solution)/shard_map/psum | solution.py:236
  1288.4 19.2 %all-reduce.26 = (bf16[768]{0:T(1024)(128)(2,1)S(1)}, bf16[768]{0:T(1024)(128)(2,1)S(1)}, bf16[768]{0:T(1024)(128)(2,1)S(1)}, bf16[768]{0:T(1024)(128)(2,1)S(1)}...) all-reduce(bf16[768]{0:T(1024)(128)(2,1)S(1)} %convert_element_type, ...), channel_id=3, replica_groups=mesh['rep'=4,'fsdp'=4,'ctx'=2] {'fsdp'}, use_global_device_ids=true, to_apply=%region_25.26.clone | all-reduce | flops 9216 | bytes 36864
  1308.3 2.5 all-reduce.29
  1310.8 10.3 all-reduce.27
  1326.2 59.5 %all-reduce.36.cloned.1.call-done = (bf16[192,2304]{1,0:T(8,128)(2,1)}, bf16[192,768]{1,0:T(8,128)(2,1)}, bf16[192,3072]{1,0:T(8,128)(2,1)}, bf16[768,768]{1,0:T(8,128)(2,1)}) async-done(((bf16[192,2304]{1,0:T(8,128)(2,1)}, bf16[192,768]{1,0:T(8,128)(2,1)}, bf16[192,3072]{1,0:T(8,128)(2,1)}, bf16[768,768]{1,0:T(8,128)(2,1)}), (bf16[192,2304]{1,0:T(8,128)(2,1)}, bf16[192,768]{1,0:T(8,128)(2,1)}, ...) | async-done | bytes 3538960 | tf_op jit(solution)/shard_map/psum | solution.py:236
  1387.6 2.6 convert_element_type.435
  (397 shorter events, 90.9 us)
Async XLA Ops:
  8.6 99.6 %copy-start.21 = (s32[1024]{0:T(1024)}, s32[1024]{0:T(1024)S(1)}, u32[]{:S(2)}) copy-start(s32[1024]{0:T(1024)S(1)} %get-tuple-element.1068) | copy-start | bytes 12292 | tf_op jit(solution)/shard_map/while
  8.6 99.6 %copy-start.41 = (pred[1024]{0:T(1024)(128)(4,1)}, pred[1024]{0:T(1024)(128)(4,1)S(1)}, u32[]{:S(2)}) copy-start(pred[1024]{0:T(1024)(128)(4,1)S(1)} %get-tuple-element.1069) | copy-start | bytes 3076 | tf_op jit(solution)/shard_map/while
  8.7 33.8 %copy-start.4 = (bf16[2,1,512,768]{3,2,1,0:T(8,128)(2,1)S(1)}, bf16[2,1,512,768]{3,2,1,0:T(8,128)(2,1)}, u32[]{:S(2)}) copy-start(bf16[2,1,512,768]{3,2,1,0:T(8,128)(2,1)} %get-tuple-element.1053) | copy-start | bytes 4718596 | tf_op jit(solution)/shard_map/while
  8.7 75.7 %all-gather.11.cloned.1.call-start = ((), (), s32[]{:S(2)}) async-start(), calls=%async_computation.11 | async-start | bytes 4423680 | tf_op jit(solution)/shard_map/while/body/eval_jaxpr/all_gather | solution.py:114
  9.4 146.6 %all-gather.9.cloned.1.call-start = ((), (), s32[]{:S(2)}) async-start(), calls=%async_computation.10 | async-start | bytes 1474560 | tf_op jit(solution)/shard_map/while/body/eval_jaxpr/all_gather | solution.py:117
  10.2 195.2 %all-gather.13.cloned.1.call-start = ((), (), s32[]{:S(2)}) async-start(), calls=%async_computation.12 | async-start | bytes 5898240 | tf_op jit(solution)/shard_map/while/body/eval_jaxpr/all_gather | solution.py:123
  10.9 283.9 %all-gather.15.cloned.1.call-start = ((), (), s32[]{:S(2)}) async-start(), calls=%async_computation.13 | async-start | bytes 5898240 | tf_op jit(solution)/shard_map/while/body/eval_jaxpr/all_gather | solution.py:163
  88.5 6.2 copy-start.40
  88.5 19.5 %copy-start.12 = (bf16[2,1,512,768]{3,2,1,0:T(8,128)(2,1)S(1)}, bf16[2,1,512,768]{3,2,1,0:T(8,128)(2,1)}, u32[]{:S(2)}) copy-start(bf16[2,1,512,768]{3,2,1,0:T(8,128)(2,1)} %get-tuple-element.1058) | copy-start | bytes 4718596 | tf_op jit(solution)/shard_map/while
  88.9 21.7 %collective-permute-start = (bf16[1,512,768]{2,1,0:T(8,128)(2,1)S(1)}, bf16[1,512,768]{2,1,0:T(8,128)(2,1)}, u32[]{:S(2)}, u32[]{:S(2)}) collective-permute-start(bf16[1,512,768]{2,1,0:T(8,128)(2,1)S(1)} %get-tuple-element.924), channel_id=1, source_target_pairs={{0,1},{2,3},{4,5},{6,7},{8,9},{10,11},{12,13},{14,15},{16,17},{18,... | collective-permute-start | bytes 2359304 | tf_op jit(solution)/shard_map/while/body/eval_jaxpr/ppermute | solution.py:14
  92.5 20.6 %collective-permute-start.1 = (bf16[1,512,768]{2,1,0:T(8,128)(2,1)}, bf16[1,512,768]{2,1,0:T(8,128)(2,1)}, u32[]{:S(2)}, u32[]{:S(2)}) collective-permute-start(bf16[1,512,768]{2,1,0:T(8,128)(2,1)} %slice.85), channel_id=1, source_target_pairs={{0,1},{2,3},{4,5},{6,7},{8,9},{10,11},{12,13},{14,15},{16,17},{18,... | collective-permute-start | bytes 2359304 | tf_op jit(solution)/shard_map/while/body/eval_jaxpr/ppermute | solution.py:14
  108.2 4.9 copy-start.23
  113.1 30.8 %copy-start = (bf16[1,1024,768]{1,2,0:T(8,128)(2,1)}, bf16[1,1024,768]{1,2,0:T(8,128)(2,1)S(1)}, u32[]{:S(2)}) copy-start(bf16[1,1024,768]{1,2,0:T(8,128)(2,1)S(1)} %copy.50) | copy-start | bytes 4718596 | tf_op jit(solution)/shard_map/while
  116.8 15.3 %copy-start.3 = (pred[512,1024]{1,0:T(8,128)(4,1)S(1)}, pred[512,1024]{1,0:T(8,128)(4,1)}, u32[]{:S(2)}) copy-start(pred[512,1024]{1,0:T(8,128)(4,1)} %fusion.200) | copy-start | bytes 1572868 | tf_op jit(solution)/shard_map/while
  159.0 135.8 %copy-start.13 = (bf16[2,1,512,768]{3,2,1,0:T(8,128)(2,1)S(1)}, bf16[2,1,512,768]{3,2,1,0:T(8,128)(2,1)}, u32[]{:S(2)}) copy-start(bf16[2,1,512,768]{3,2,1,0:T(8,128)(2,1)} %get-tuple-element.1058) | copy-start | bytes 4718596 | tf_op jit(solution)/shard_map/while
  294.8 9.3 copy-start.43
  312.5 13.6 copy-start.1
  312.5 13.6 copy-start.2
  442.8 14.2 %copy-start.9 = (bf16[512,3072]{1,0:T(8,128)(2,1)S(1)}, bf16[512,3072]{1,0:T(8,128)(2,1)}, u32[]{:S(2)}) copy-start(bf16[512,3072]{1,0:T(8,128)(2,1)} %copy-done.8) | copy-start | bytes 9437188 | tf_op jit(solution)/shard_map/while
  455.7 20.5 %collective-permute-start.2 = (bf16[1,512,768]{1,2,0:T(8,128)(2,1)}, bf16[1,512,768]{1,2,0:T(8,128)(2,1)}, u32[]{:S(2)}, u32[]{:S(2)}) collective-permute-start(bf16[1,512,768]{1,2,0:T(8,128)(2,1)} %slice.86), channel_id=1, source_target_pairs={{1,0},{3,2},{5,4},{7,6},{9,8},{11,10},{13,12},{15,14},{17,16},{19,... | collective-permute-start | bytes 2359304 | tf_op jit(solution)/shard_map/while/body/eval_jaxpr/ppermute | solution.py:14
  464.2 14.9 %collective-permute-start.3 = (bf16[1,512,768]{1,2,0:T(8,128)(2,1)S(1)}, bf16[1,512,768]{1,2,0:T(8,128)(2,1)S(1)}, u32[]{:S(2)}, u32[]{:S(2)}) collective-permute-start(bf16[1,512,768]{1,2,0:T(8,128)(2,1)S(1)} %slice.87), channel_id=1, source_target_pairs={{1,0},{3,2},{5,4},{7,6},{9,8},{11,10},{13,12},{15,14},{17,16},{19,... | collective-permute-start | bytes 2359304 | tf_op jit(solution)/shard_map/while/body/eval_jaxpr/ppermute | solution.py:14
  465.5 9.2 copy-start.6
  465.6 9.2 copy-start.15
  479.2 7.9 copy-start.35
  479.8 7.3 copy-start.44
  492.3 96.5 %copy-start.21 = (s32[1024]{0:T(1024)}, s32[1024]{0:T(1024)S(1)}, u32[]{:S(2)}) copy-start(s32[1024]{0:T(1024)S(1)} %get-tuple-element.1068) | copy-start | bytes 12292 | tf_op jit(solution)/shard_map/while
  492.4 96.5 %copy-start.41 = (pred[1024]{0:T(1024)(128)(4,1)}, pred[1024]{0:T(1024)(128)(4,1)S(1)}, u32[]{:S(2)}) copy-start(pred[1024]{0:T(1024)(128)(4,1)S(1)} %get-tuple-element.1069) | copy-start | bytes 3076 | tf_op jit(solution)/shard_map/while
  492.4 28.6 %copy-start.4 = (bf16[2,1,512,768]{3,2,1,0:T(8,128)(2,1)S(1)}, bf16[2,1,512,768]{3,2,1,0:T(8,128)(2,1)}, u32[]{:S(2)}) copy-start(bf16[2,1,512,768]{3,2,1,0:T(8,128)(2,1)} %get-tuple-element.1053) | copy-start | bytes 4718596 | tf_op jit(solution)/shard_map/while
  492.4 72.6 %all-gather.11.cloned.1.call-start = ((), (), s32[]{:S(2)}) async-start(), calls=%async_computation.11 | async-start | bytes 4423680 | tf_op jit(solution)/shard_map/while/body/eval_jaxpr/all_gather | solution.py:114
  493.0 143.5 %all-gather.9.cloned.1.call-start = ((), (), s32[]{:S(2)}) async-start(), calls=%async_computation.10 | async-start | bytes 1474560 | tf_op jit(solution)/shard_map/while/body/eval_jaxpr/all_gather | solution.py:117
  493.6 192.6 %all-gather.13.cloned.1.call-start = ((), (), s32[]{:S(2)}) async-start(), calls=%async_computation.12 | async-start | bytes 5898240 | tf_op jit(solution)/shard_map/while/body/eval_jaxpr/all_gather | solution.py:123
  494.3 281.4 %all-gather.15.cloned.1.call-start = ((), (), s32[]{:S(2)}) async-start(), calls=%async_computation.13 | async-start | bytes 5898240 | tf_op jit(solution)/shard_map/while/body/eval_jaxpr/all_gather | solution.py:163
  569.2 6.2 copy-start.40
  569.2 19.5 %copy-start.12 = (bf16[2,1,512,768]{3,2,1,0:T(8,128)(2,1)S(1)}, bf16[2,1,512,768]{3,2,1,0:T(8,128)(2,1)}, u32[]{:S(2)}) copy-start(bf16[2,1,512,768]{3,2,1,0:T(8,128)(2,1)} %get-tuple-element.1058) | copy-start | bytes 4718596 | tf_op jit(solution)/shard_map/while
  569.5 21.7 %collective-permute-start = (bf16[1,512,768]{2,1,0:T(8,128)(2,1)S(1)}, bf16[1,512,768]{2,1,0:T(8,128)(2,1)}, u32[]{:S(2)}, u32[]{:S(2)}) collective-permute-start(bf16[1,512,768]{2,1,0:T(8,128)(2,1)S(1)} %get-tuple-element.924), channel_id=1, source_target_pairs={{0,1},{2,3},{4,5},{6,7},{8,9},{10,11},{12,13},{14,15},{16,17},{18,... | collective-permute-start | bytes 2359304 | tf_op jit(solution)/shard_map/while/body/eval_jaxpr/ppermute | solution.py:14
  573.2 20.3 %collective-permute-start.1 = (bf16[1,512,768]{2,1,0:T(8,128)(2,1)}, bf16[1,512,768]{2,1,0:T(8,128)(2,1)}, u32[]{:S(2)}, u32[]{:S(2)}) collective-permute-start(bf16[1,512,768]{2,1,0:T(8,128)(2,1)} %slice.85), channel_id=1, source_target_pairs={{0,1},{2,3},{4,5},{6,7},{8,9},{10,11},{12,13},{14,15},{16,17},{18,... | collective-permute-start | bytes 2359304 | tf_op jit(solution)/shard_map/while/body/eval_jaxpr/ppermute | solution.py:14
  588.8 4.7 copy-start.23
  593.5 30.9 %copy-start = (bf16[1,1024,768]{1,2,0:T(8,128)(2,1)}, bf16[1,1024,768]{1,2,0:T(8,128)(2,1)S(1)}, u32[]{:S(2)}) copy-start(bf16[1,1024,768]{1,2,0:T(8,128)(2,1)S(1)} %copy.50) | copy-start | bytes 4718596 | tf_op jit(solution)/shard_map/while
  597.2 15.3 %copy-start.3 = (pred[512,1024]{1,0:T(8,128)(4,1)S(1)}, pred[512,1024]{1,0:T(8,128)(4,1)}, u32[]{:S(2)}) copy-start(pred[512,1024]{1,0:T(8,128)(4,1)} %fusion.200) | copy-start | bytes 1572868 | tf_op jit(solution)/shard_map/while
  639.5 136.2 %copy-start.13 = (bf16[2,1,512,768]{3,2,1,0:T(8,128)(2,1)S(1)}, bf16[2,1,512,768]{3,2,1,0:T(8,128)(2,1)}, u32[]{:S(2)}) copy-start(bf16[2,1,512,768]{3,2,1,0:T(8,128)(2,1)} %get-tuple-element.1058) | copy-start | bytes 4718596 | tf_op jit(solution)/shard_map/while
  775.7 9.7 copy-start.43
  793.8 13.6 copy-start.1
  793.8 13.6 copy-start.2
  923.9 17.0 %copy-start.9 = (bf16[512,3072]{1,0:T(8,128)(2,1)S(1)}, bf16[512,3072]{1,0:T(8,128)(2,1)}, u32[]{:S(2)}) copy-start(bf16[512,3072]{1,0:T(8,128)(2,1)} %copy-done.8) | copy-start | bytes 9437188 | tf_op jit(solution)/shard_map/while
  939.6 22.8 %collective-permute-start.2 = (bf16[1,512,768]{1,2,0:T(8,128)(2,1)}, bf16[1,512,768]{1,2,0:T(8,128)(2,1)}, u32[]{:S(2)}, u32[]{:S(2)}) collective-permute-start(bf16[1,512,768]{1,2,0:T(8,128)(2,1)} %slice.86), channel_id=1, source_target_pairs={{1,0},{3,2},{5,4},{7,6},{9,8},{11,10},{13,12},{15,14},{17,16},{19,... | collective-permute-start | bytes 2359304 | tf_op jit(solution)/shard_map/while/body/eval_jaxpr/ppermute | solution.py:14
  950.3 14.9 %collective-permute-start.3 = (bf16[1,512,768]{1,2,0:T(8,128)(2,1)S(1)}, bf16[1,512,768]{1,2,0:T(8,128)(2,1)S(1)}, u32[]{:S(2)}, u32[]{:S(2)}) collective-permute-start(bf16[1,512,768]{1,2,0:T(8,128)(2,1)S(1)} %slice.87), channel_id=1, source_target_pairs={{1,0},{3,2},{5,4},{7,6},{9,8},{11,10},{13,12},{15,14},{17,16},{19,... | collective-permute-start | bytes 2359304 | tf_op jit(solution)/shard_map/while/body/eval_jaxpr/ppermute | solution.py:14
  951.6 9.2 copy-start.6
  951.7 9.2 copy-start.15
  965.3 10.1 copy-start.35
  965.9 9.5 copy-start.44
  983.9 32.7 %reduce-scatter.7.cloned.1.call-start = ((), (), s32[]{:S(2)}) async-start(), calls=%async_computation.5 | async-start | bytes 1474560 | tf_op jit(solution)/shard_map/reduce_scatter | solution.py:231
  986.8 97.0 %reduce-scatter.5.cloned.1.call-start = ((), (), s32[]{:S(2)}) async-start(), calls=%async_computation.4 | async-start | bytes 4423680 | tf_op jit(solution)/shard_map/reduce_scatter | solution.py:231
  992.0 179.3 %reduce-scatter.9.cloned.1.call-start = ((), (), s32[]{:S(2)}) async-start(), calls=%async_computation.6 | async-start | bytes 5898240 | tf_op jit(solution)/shard_map/reduce_scatter | solution.py:231
  998.8 260.5 %reduce-scatter.11.cloned.1.call-start = ((), (), s32[]{:S(2)}) async-start(), calls=%async_computation.7 | async-start | bytes 5898240 | tf_op jit(solution)/shard_map/reduce_scatter | solution.py:231
  1005.3 281.1 %all-reduce.38.cloned.1.call-start = ((), (), s32[]{:S(2)}) async-start(), calls=%async_computation.9 | async-start | bytes 7077888 | tf_op jit(solution)/shard_map/psum | solution.py:236
  1259.3 27.0 %copy-start.49 = (u32[32]{0:T(128)S(1)}, u32[32]{0:T(128)}, u32[]{:S(2)}) copy-start(u32[32]{0:T(128)} %get-tuple-element.1147) | copy-start | bytes 388
  1259.3 28.9 %copy-start.39 = (f32[768]{0:T(1024)S(1)}, f32[768]{0:T(1024)}, u32[]{:S(2)}) copy-start(f32[768]{0:T(1024)} %get-tuple-element.421) | copy-start | bytes 9220
  1259.3 29.0 %copy-start.36 = (f32[768]{0:T(1024)S(1)}, f32[768]{0:T(1024)}, u32[]{:S(2)}) copy-start(f32[768]{0:T(1024)} %get-tuple-element.422) | copy-start | bytes 9220
  1259.3 29.0 %copy-start.33 = (f32[768]{0:T(1024)S(1)}, f32[768]{0:T(1024)}, u32[]{:S(2)}) copy-start(f32[768]{0:T(1024)} %get-tuple-element.424) | copy-start | bytes 9220
  1259.3 29.0 %copy-start.30 = (f32[768]{0:T(1024)S(1)}, f32[768]{0:T(1024)}, u32[]{:S(2)}) copy-start(f32[768]{0:T(1024)} %get-tuple-element.425) | copy-start | bytes 9220
  1259.3 29.0 %copy-start.27 = (f32[768]{0:T(1024)S(1)}, f32[768]{0:T(1024)}, u32[]{:S(2)}) copy-start(f32[768]{0:T(1024)} %get-tuple-element.426) | copy-start | bytes 9220
  1259.4 29.1 %copy-start.20 = (f32[3072]{0:T(1024)S(1)}, f32[3072]{0:T(1024)}, u32[]{:S(2)}) copy-start(f32[3072]{0:T(1024)} %get-tuple-element.430) | copy-start | bytes 36868
  1259.4 126.3 %all-reduce.36.cloned.1.call-start = ((), (), s32[]{:S(2)}) async-start(), calls=%async_computation.8 | async-start | bytes 7077888 | tf_op jit(solution)/shard_map/psum | solution.py:236
  1385.7 4.5 copy-start.17
  (49 other events, 121.2 us)
Sparse Core Ops, SparseCore 0:
  11.2 73.1 all-gather.10
  86.0 29.1 all-gather.8
  116.8 88.5 all-gather.12
  206.9 87.8 all-gather.14
  494.6 70.4 all-gather.10
  566.5 29.3 all-gather.8
  597.6 88.5 all-gather.12
  687.8 87.8 all-gather.14
Sparse Core Ops, SparseCore 1:
  987.3 29.2 reduce-scatter.6
  1018.7 65.0 reduce-scatter.4
  1085.9 85.3 reduce-scatter.8
  1173.6 85.6 reduce-scatter.10
  1261.9 24.4 all-reduce.37
  1290.2 95.4 all-reduce.35
